TPU v7x, 512 devices: a whole 4x8x8 slice. The times are simulated.
512 devices in a mesh: cfg: 2 (over z_lo), rs: 32 (over x, z_hi, core), tp: 8 (over y).
Axes of the slice: x: 4, y: 8, z: 8 (z_hi: 4, z_lo: 2; z = z_hi * 2 + z_lo), core: 2. Of those that a mesh axis runs over, the one named last changes fastest.
Arguments:
- latents: float32 [8192, 2, 16], P('rs'), may hold values from -6 to 6
- timesteps: int32 [8, 2], replicated, may hold values from 0 to 249
- labels: int32 [8, 2], replicated, may hold values from 0 to 999
- solver_table: float32 [250, 2], replicated, may hold values from 0.5 to 1.5
- time_table: bfloat16 [250, 1152], P(None, 'tp'), may hold values from -6 to 6
- label_table: bfloat16 [1001, 1152], P(None, 'tp'), may hold values from -6 to 6
- patch_weight: bfloat16 [16, 1152], replicated, may hold values from -1.5 to 1.5
- patch_bias: float32 [1152], replicated, may hold values from -3 to 3
- modulation_weight: bfloat16 [9216, 1152], P(('rs', 'tp')), may hold values from -0.1875 to 0.1875
- modulation_bias: float32 [9216], P(('rs', 'tp')), may hold values from -3 to 3
- heads_weight: bfloat16 [1, 1152, 3, 1152], P(None, None, None, 'tp'), may hold values from -0.375 to 0.375
- heads_bias: float32 [1, 3, 1152], P(None, None, 'tp'), may hold values from -1.75 to 1.75
- output_weight: bfloat16 [1, 1152, 1152], P(None, 'tp'), may hold values from -0.1875 to 0.1875
- output_bias: float32 [1, 1152], replicated, may hold values from -1.75 to 1.75
- up_weight: bfloat16 [1, 1152, 4608], P(None, None, 'tp'), may hold values from -0.1875 to 0.1875
- up_bias: float32 [1, 4608], P(None, 'tp'), may hold values from -1.75 to 1.75
- down_weight: bfloat16 [1, 4608, 1152], P(None, 'tp'), may hold values from -0.09375 to 0.09375
- down_bias: float32 [1, 1152], replicated, may hold values from -1.75 to 1.75
- final_weight: bfloat16 [1152, 16], replicated, may hold values from -0.1875 to 0.1875
- final_bias: float32 [16], replicated, may hold values from -1.75 to 1.75
Outputs:
- next_latents: float32 [8192, 2, 16], P(('rs', 'tp'), None, 'cfg')
All inputs are finite; a program needn't handle non-finite values.
Results may differ from a plain program's by a relative error of at most 0.02.
Values may be sent and summed in bfloat16 or wider, within the bound.
A program may use at most 64 MiB of HBM per device.

v0:
```python
import jax
import jax.numpy as jnp
from jax import lax
from jax.sharding import PartitionSpec as P

HEAD_DIM = 72
GRID = 32
LAYERS = 1
guidance = 4.0


def partner_2(value, axis, stride):
    mask = 2**stride
    pairs = [(source, source ^ mask) for source in range(lax.axis_size(axis))]
    return lax.ppermute(value, axis, pairs)


def layer_norm(values):
    centre = values - jnp.mean(values, axis=-1, keepdims=True)
    spread = jnp.mean(centre * centre, axis=-1, keepdims=True)
    return centre * lax.rsqrt(spread + 1e-06)


def position_rows(token_index, grid_side, model_width):
    freq_count = model_width // 4
    frequency = 1.0 / 10000.0 ** (jnp.arange(freq_count, dtype=jnp.float32) / freq_count)
    row_angle = (token_index // grid_side).astype(jnp.float32)[:, None] * frequency[None, :]
    col_angle = (token_index % grid_side).astype(jnp.float32)[:, None] * frequency[None, :]
    return jnp.concatenate(
        [jnp.sin(row_angle), jnp.cos(row_angle), jnp.sin(col_angle), jnp.cos(col_angle)], axis=1
    )


def modulate(stream, modulation, offset):
    return (
        layer_norm(stream) * (1.0 + modulation[None, :, offset + 1]) + modulation[None, :, offset]
    ).astype(jnp.bfloat16)


def project_heads(normed, weight, bias):
    row_count, latents_dev, model_width = normed.shape
    flattened = normed.reshape(row_count * latents_dev, model_width)
    result = jnp.dot(
        flattened, weight.reshape(model_width, -1), preferred_element_type=jnp.float32
    ) + bias.reshape(-1)
    return result.astype(jnp.bfloat16).reshape(row_count, latents_dev, -1)


def hidden_units(normed, weight, bias):
    row_count, latents_dev, model_width = normed.shape
    flattened = normed.reshape(row_count * latents_dev, model_width)
    preact = jnp.dot(flattened, weight, preferred_element_type=jnp.float32) + bias
    return (
        jax.nn.gelu(preact, approximate=True)
        .astype(jnp.bfloat16)
        .reshape(row_count, latents_dev, -1)
    )


def attend_block(queries, key_block, columns):
    key_count, latents_dev = (key_block.shape[0], key_block.shape[1])
    head_count, head_size = (queries.shape[2], queries.shape[3])
    key_rows = key_block[..., :columns].reshape(key_count, latents_dev, head_count, head_size)
    value_rows = key_block[..., columns:].reshape(key_count, latents_dev, head_count, head_size)
    scores = jnp.einsum(
        "qlhd,klhd->lhqk", queries, key_rows, preferred_element_type=jnp.float32
    ) * head_size ** (-0.5)
    row_top = jnp.max(scores, axis=-1)
    exponent = jnp.exp(scores - row_top[..., None])
    row_total = jnp.sum(exponent, axis=-1)
    weighted = jnp.einsum(
        "lhqk,klhd->lhqd",
        exponent.astype(jnp.bfloat16),
        value_rows,
        preferred_element_type=jnp.float32,
    )
    return (row_top, row_total, weighted)


def merge_blocks(first, second):
    row_top = jnp.maximum(first[0], second[0])
    left_scale = jnp.exp(first[0] - row_top)
    right_scale = jnp.exp(second[0] - row_top)
    row_total = first[1] * left_scale + second[1] * right_scale
    weighted = first[2] * left_scale[..., None] + second[2] * right_scale[..., None]
    return (row_top, row_total, weighted)


def attention(projected, columns, head_size):
    row_count, latents_dev = (projected.shape[0], projected.shape[1])
    queries = projected[..., :columns].reshape(
        row_count, latents_dev, columns // head_size, head_size
    )
    own_block = projected[..., columns:]
    running = attend_block(queries, own_block, columns)
    near_block = partner_2(own_block, "rs", 0)
    running = merge_blocks(running, attend_block(queries, near_block, columns))
    far_block = partner_2(jnp.concatenate([own_block, near_block], axis=0), "rs", 1)
    running = merge_blocks(running, attend_block(queries, far_block, columns))
    result = running[2] / running[1][..., None]
    return (
        jnp.transpose(result, (2, 0, 1, 3))
        .reshape(row_count, latents_dev, columns)
        .astype(jnp.bfloat16)
    )


def per_device(
    latents,
    timesteps,
    labels,
    solver_table,
    time_table,
    label_table,
    patch_weight,
    patch_bias,
    modulation_weight,
    modulation_bias,
    heads_weight,
    heads_bias,
    output_weight,
    output_bias,
    up_weight,
    up_bias,
    down_weight,
    down_bias,
    final_weight,
    final_bias,
):
    tp_count = lax.axis_size("tp")
    tp_index = lax.axis_index("tp")
    half_index = lax.axis_index("cfg")
    rs_index = lax.axis_index("rs")
    group_index = rs_index // 4
    quarter = rs_index % 4
    local_tokens, latents_dev, patch_width = latents.shape
    model_width = patch_weight.shape[1]
    share_rows = local_tokens // tp_count
    classes = label_table.shape[0] - 1
    columns = heads_weight.shape[3]
    steps_all = timesteps.reshape(-1)
    class_ids = jnp.where(half_index == 0, labels.reshape(-1), classes)
    step_onehot = jax.nn.one_hot(steps_all, time_table.shape[0], dtype=jnp.bfloat16)
    class_onehot = jax.nn.one_hot(class_ids, classes + 1, dtype=jnp.bfloat16)
    condition_part = jnp.dot(step_onehot, time_table, preferred_element_type=jnp.float32) + jnp.dot(
        class_onehot, label_table, preferred_element_type=jnp.float32
    )
    condition = lax.all_gather(condition_part, "tp", axis=1, tiled=True)
    activation = jax.nn.silu(condition).astype(jnp.bfloat16)
    modulation_part = (
        lax.dot_general(
            activation,
            modulation_weight,
            (((1,), (1,)), ((), ())),
            preferred_element_type=jnp.float32,
        )
        + modulation_bias
    )
    modulation_all = lax.all_gather(modulation_part, ("rs", "tp"), axis=1, tiled=True)
    modulation_all = modulation_all.reshape(timesteps.shape[0], latents_dev, -1, model_width)
    modulation = lax.dynamic_index_in_dim(modulation_all, group_index, 0, keepdims=False)
    token_index = quarter * local_tokens + jnp.arange(local_tokens, dtype=jnp.int32)
    position = position_rows(token_index, GRID, model_width)
    own_latents = lax.dynamic_slice_in_dim(latents, tp_index * share_rows, share_rows, 0)
    flattened = latents.reshape(-1, patch_width).astype(jnp.bfloat16)
    embedded = jnp.dot(flattened, patch_weight, preferred_element_type=jnp.float32) + patch_bias
    stream = embedded.reshape(latents.shape[0], latents_dev, model_width) + position[:, None, :]
    projected = project_heads(modulate(stream, modulation, 0), heads_weight[0], heads_bias[0])
    attended = attention(projected, columns, HEAD_DIM).reshape(-1, columns)
    head_terms = jnp.dot(attended, output_weight[0], preferred_element_type=jnp.float32)
    attn_out = (
        lax.psum(head_terms.astype(jnp.bfloat16), "tp")
        .astype(jnp.float32)
        .reshape(local_tokens, latents_dev, model_width)
    )
    stream = stream + modulation[None, :, 2] * (attn_out + output_bias[0])
    hidden = hidden_units(modulate(stream, modulation, 3), up_weight[0], up_bias[0])
    unit_terms = jnp.dot(
        hidden.reshape(-1, hidden.shape[2]), down_weight[0], preferred_element_type=jnp.float32
    )
    mlp_out = (
        lax.psum(unit_terms.astype(jnp.bfloat16), "tp")
        .astype(jnp.float32)
        .reshape(local_tokens, latents_dev, model_width)
    )
    stream = stream + modulation[None, :, 5] * (mlp_out + down_bias[0])
    own_stream = lax.dynamic_slice_in_dim(stream, tp_index * share_rows, share_rows, 0)
    final_normed = modulate(own_stream, modulation, 6 * LAYERS)
    noise_pred = (
        jnp.dot(
            final_normed.reshape(-1, model_width), final_weight, preferred_element_type=jnp.float32
        )
        + final_bias
    )
    noise_pred = noise_pred.reshape(share_rows, latents_dev, patch_width)
    half_width = patch_width // 2
    kept_half = lax.dynamic_slice_in_dim(noise_pred, half_index * half_width, half_width, 2)
    sent_half = lax.dynamic_slice_in_dim(noise_pred, (1 - half_index) * half_width, half_width, 2)
    partner = partner_2(sent_half, "cfg", 0)
    conditional = jnp.where(half_index == 0, kept_half, partner)
    unconditional = jnp.where(half_index == 0, partner, kept_half)
    guided = unconditional + guidance * (conditional - unconditional)
    own_channels = lax.dynamic_slice_in_dim(own_latents, half_index * half_width, half_width, 2)
    step_own = lax.dynamic_index_in_dim(timesteps, group_index, 0, keepdims=False)
    step_hot_own = jax.nn.one_hot(step_own, solver_table.shape[0], dtype=jnp.float32)
    coefficients = jnp.dot(step_hot_own, solver_table, precision=lax.Precision.HIGHEST)
    return coefficients[None, :, 0:1] * own_channels + coefficients[None, :, 1:2] * guided


def solution(mesh):
    in_specs = (
        P("rs", None, None),
        P(),
        P(),
        P(),
        P(None, "tp"),
        P(None, "tp"),
        P(),
        P(),
        P(("rs", "tp"), None),
        P(("rs", "tp")),
        P(None, None, None, "tp"),
        P(None, None, "tp"),
        P(None, "tp", None),
        P(),
        P(None, None, "tp"),
        P(None, "tp"),
        P(None, "tp", None),
        P(),
        P(),
        P(),
    )
    out_specs = P(("rs", "tp"), None, "cfg")
    return jax.shard_map(
        per_device, mesh=mesh, in_specs=in_specs, out_specs=out_specs, check_vma=False
    )
```

profile of v0, /device:TPU:2, one launch (start us, length us, event | category | flops | bytes accessed | tf_op | source)
XLA Modules:
  0.0 997.7 jit_solution(18414856131837989022)
XLA Ops:
  6.6 3.8 multiply_cosine_fusion
  10.4 1.6 concatenate.6
  12.0 2.2 add.308
  14.2 4.0 add.314
  18.4 3.6 fusion.90
  22.1 1.4 copy-done.1
  24.6 26.2 %all-gather = f32[8,144,16]{1,2,0:T(8,128)S(1)} all-gather(f32[1,144,16]{1,2,0:T(8,128)S(1)} %fusion.29), channel_id=1, replica_groups=mesh['cfg'=2,'rs'=32,'tp'=8] {'tp'}, dimensions={0}, use_global_device_ids=true | all-gather | bytes 82944 | tf_op jit(solution)/shard_map/all_gather | solution.py:148
  51.2 616.4 %all-gather.1 = f32[256,36,16]{1,2,0:T(8,128)S(1)} all-gather(f32[1,36,16]{1,2,0:T(8,128)S(1)} %fusion.30), channel_id=1, replica_groups=mesh['cfg'=2,'rs'=32,'tp'=8] {'rs','tp'}, dimensions={0}, use_global_device_ids=true | all-gather | bytes 592128 | tf_op jit(solution)/shard_map/all_gather | solution.py:159
  667.6 0.7 copy.75
  668.3 2.4 reshape.290
  670.7 1.2 copy.101
  672.6 2.1 add.320
  674.7 4.0 add.321
  678.7 2.1 mul.284
  680.8 4.1 mul.285
  685.0 4.1 fusion.4
  690.2 1.9 collective-permute-start
  692.1 0.8 fusion.92
  692.9 0.8 copy.78
  694.1 1.3 fusion.95
  695.4 0.8 fusion.34
  696.1 2.2 pad_maximum_fusion
  698.3 2.0 copy.84
  700.4 2.1 collective-permute-start.1
  702.5 1.5 fusion.93
  704.2 0.8 copy.82
  705.6 26.2 %collective-permute-done.1 = bf16[512,2,288]{0,2,1:T(8,128)(2,1)} collective-permute-done((bf16[512,2,288]{0,2,1:T(8,128)(2,1)}, bf16[512,2,288]{0,2,1:T(8,128)(2,1)}, u32[]{:S(2)}, u32[]{:S(2)}) %collective-permute-start.1) | collective-permute-done | bytes 589856 | tf_op jit(solution)/shard_map/ppermute | solution.py:15
  731.8 1.1 fusion.91
  735.8 1.5 convolution_convert_fusion
  737.4 2.1 mul.280
  739.4 4.1 mul.306
  743.5 2.1 add.341
  745.6 4.0 add.342
  749.7 2.0 mul.311
  751.7 4.1 mul.312
  755.7 133.0 %all-reduce.3.cloned.1.call-done = bf16[512,1152]{1,0:T(8,128)(2,1)} async-done(((bf16[512,1152]{1,0:T(8,128)(2,1)}), bf16[512,1152]{1,0:T(8,128)(2,1)}) %all-reduce.3.cloned.1.call-update) | async-done | bytes 1179664 | tf_op jit(solution)/shard_map/psum | solution.py:172
  888.8 3.2 fusion.85
  891.9 1.4 copy-done.2
  893.7 5.7 convolution_convert_fusion.1
  899.5 1.3 reshape.283
  901.0 4.1 reshape.272
  905.3 0.9 constant_dynamic-slice_fusion.2
  906.3 2.2 reshape.282
  908.5 73.4 %all-reduce.5.cloned.1.call-done = bf16[256,2,1152]{2,1,0:T(2,128)(2,1)} async-done(((bf16[256,2,1152]{2,1,0:T(2,128)(2,1)}), bf16[256,2,1152]{2,1,0:T(2,128)(2,1)}) %all-reduce.5.cloned.1.call-update) | async-done | bytes 1179664 | tf_op jit(solution)/shard_map/psum | solution.py:182
  981.9 1.6 fusion.83
  984.7 3.6 collective-permute-start.2
  988.5 1.7 collective-permute-done.2
  990.2 0.7 multiply_add_fusion.1
  (120 shorter events, 9.7 us)
Async XLA Ops:
  6.5 887.2 %copy-start = (bf16[1,576,1152]{2,1,0:T(8,128)(2,1)S(1)}, bf16[1,576,1152]{2,1,0:T(8,128)(2,1)}, u32[]{:S(2)}) copy-start(bf16[1,576,1152]{2,1,0:T(8,128)(2,1)} %param.36) | copy-start | bytes 3981316
  6.5 882.2 %all-reduce.3.cloned.1.call-start = ((), (), s32[]{:S(2)}) async-start(), calls=%async_computation | async-start | bytes 2359296 | tf_op jit(solution)/shard_map/psum | solution.py:172
  12.0 6.3 copy-start.3
  14.2 4.1 copy-start.10
  14.2 4.2 copy-start.11
  14.2 4.2 copy-start.14
  22.1 1.4 copy-start.1
  22.1 1.8 copy-start.21
  22.1 2.0 copy-start.17
  22.1 2.2 copy-start.23
  22.1 2.3 copy-start.8
  22.1 28.9 %copy-start.22 = (bf16[36,1152]{1,0:T(8,128)(2,1)S(1)}, bf16[36,1152]{1,0:T(8,128)(2,1)}, u32[]{:S(2)}) copy-start(bf16[36,1152]{1,0:T(8,128)(2,1)} %param.28) | copy-start | bytes 248836
  22.1 28.9 %copy-start.26 = (f32[36]{0:T(128)S(1)}, f32[36]{0:T(128)}, u32[]{:S(2)}) copy-start(f32[36]{0:T(128)} %param.29) | copy-start | bytes 436
  680.8 4.1 copy-start.19
  680.8 4.2 copy-start.6
  690.2 5.9 copy-start.5
  690.2 5.9 collective-permute-start
  700.4 31.5 %collective-permute-start.1 = (bf16[512,2,288]{0,2,1:T(8,128)(2,1)}, bf16[512,2,288]{0,2,1:T(8,128)(2,1)}, u32[]{:S(2)}, u32[]{:S(2)}) collective-permute-start(bf16[512,2,288]{0,2,1:T(8,128)(2,1)} %copy.84), channel_id=1, source_target_pairs={{0,16},{8,24},{16,0},{24,8},{32,48},{40,56},{48,32},{56,40},{64,80... | collective-permute-start | bytes 1769480 | tf_op jit(solution)/shard_map/ppermute | solution.py:15
  732.9 1.2 copy-start.13
  734.1 1.0 copy-start.9
  734.5 1.3 copy-start.7
  737.3 244.6 %all-reduce.5.cloned.1.call-start = ((), (), s32[]{:S(2)}) async-start(), calls=%async_computation.1 | async-start | bytes 2359296 | tf_op jit(solution)/shard_map/psum | solution.py:182
  739.4 4.1 copy-start.15
  739.4 4.1 copy-start.12
  751.7 4.1 copy-start.20
  891.9 1.4 copy-start.2
  899.5 1.4 copy-start.18
  901.0 4.1 copy-start.16
  901.0 4.1 copy-start.25
  901.0 5.2 copy-start.4
  906.3 77.9 %copy-start.24 = (bf16[1152,16]{0,1:T(8,128)(2,1)S(1)}, bf16[1152,16]{0,1:T(8,128)(2,1)}, u32[]{:S(2)}) copy-start(bf16[1152,16]{0,1:T(8,128)(2,1)} %param.38) | copy-start | bytes 110596
  906.3 77.9 %copy-start.27 = (f32[16]{0:T(128)S(1)}, f32[16]{0:T(128)}, u32[]{:S(2)}) copy-start(f32[16]{0:T(128)} %param.39) | copy-start | bytes 196
  984.7 5.5 collective-permute-start.2
Sparse Core Ops, SparseCore 0:
  737.4 151.2 all-reduce.2
  900.9 80.9 all-reduce.4
where the time goes:
time: 999 us; the launch traced here: 998 us
  blocking collectives  643 us (64%)
  waiting for transfers between devices  234 us (23%)
  local copies, waits for them, and re-layouts  64.7 us (6%)
  matrix products  19.2 us (2%)
  other arithmetic  15.1 us (2%)
  between operations  14 us (1%)
    all_gather x1, blocking collectives, per_device(): lax.all_gather(modulation_part, ('rs', 'tp'), axis=1, tiled=True)  616 us
    psum x1, waiting for transfers between devices, per_device(): lax.psum(head_terms.astype(jnp.bfloat16), 'tp').astype(jnp.float32)  133 us
    psum x1, waiting for transfers between devices, per_device(): lax.psum(unit_terms.astype(jnp.bfloat16), 'tp').astype(jnp.float32)  73.4 us
    ppermute x3, waiting for transfers between devices, partner_2(): return lax.ppermute(value, axis, pairs)  28 us
    all_gather x1, blocking collectives, per_device(): condition = lax.all_gather(condition_part, 'tp', axis=1, tiled=True)  26.2 us
  transfers between devices with their start and end apart: 5, of which 4 were waited for; matrix products, arithmetic and copies ran while one was open for 3% of the time, Pallas kernels for 0%

commit v1 on v0

--- a/solution.py
+++ b/solution.py
@@ -127,6 +127,10 @@
     final_weight,
     final_bias,
 ):
+
+    def divide_plate_by_axis(matrix):
+        return jnp.sum(jax.lax.all_gather(matrix, axis_name="tp"), axis=0)
+
     tp_count = lax.axis_size("tp")
     tp_index = lax.axis_index("tp")
     half_index = lax.axis_index("cfg")
@@ -179,7 +183,7 @@
         hidden.reshape(-1, hidden.shape[2]), down_weight[0], preferred_element_type=jnp.float32
     )
     mlp_out = (
-        lax.psum(unit_terms.astype(jnp.bfloat16), "tp")
+        divide_plate_by_axis(unit_terms.astype(jnp.bfloat16))
         .astype(jnp.float32)
         .reshape(local_tokens, latents_dev, model_width)
     )

time: 999 us -> 1030 us (1.031)
  waiting for transfers between devices: 234 us -> 259 us
    all_gather x0 -> x1, waiting for transfers between devices: none -> 97.9 us  [divide_plate_by_axis(): return jnp.sum(jax.lax.all_gather(matrix, axis_name='tp'), axis=0)]
    psum x1 -> x0, waiting for transfers between devices: 73.4 us -> none  [per_device(): lax.psum(unit_terms.astype(jnp.bfloat16), 'tp').astype(jnp.float32)]
where the time goes in v1:
time: 1030 us
  blocking collectives  643 us (62%)
  waiting for transfers between devices  259 us (25%)
  local copies, waits for them, and re-layouts  66 us (6%)
  other arithmetic  20.8 us (2%)
  matrix products  20 us (2%)
  between operations  14 us (1%)
    all_gather x1, blocking collectives, per_device(): lax.all_gather(modulation_part, ('rs', 'tp'), axis=1, tiled=True)  616 us
    psum x1, waiting for transfers between devices, per_device(): lax.psum(head_terms.astype(jnp.bfloat16), 'tp').astype(jnp.float32)  133 us
    all_gather x1, waiting for transfers between devices, divide_plate_by_axis(): return jnp.sum(jax.lax.all_gather(matrix, axis_name='tp'), axis=0)  97.9 us
    ppermute x3, waiting for transfers between devices, partner_2(): return lax.ppermute(value, axis, pairs)  28 us
    all_gather x1, blocking collectives, per_device(): condition = lax.all_gather(condition_part, 'tp', axis=1, tiled=True)  26.2 us
  transfers between devices with their start and end apart: 5, of which 4 were waited for; matrix products, arithmetic and copies ran while one was open for 3% of the time, Pallas kernels for 0%

profile of v1, /device:TPU:2, one launch (start us, length us, event | category | flops | bytes accessed | tf_op | source)
XLA Modules:
  0.0 1030.0 jit_solution(2793520905622703950)
XLA Ops:
  6.6 3.8 multiply_cosine_fusion
  10.4 1.6 concatenate.6
  12.0 2.2 add.306
  14.2 4.0 add.312
  18.4 3.6 fusion.91
  22.1 1.4 copy-done.1
  24.6 26.2 %all-gather.1 = f32[8,144,16]{1,2,0:T(8,128)S(1)} all-gather(f32[1,144,16]{1,2,0:T(8,128)S(1)} %fusion.29), channel_id=1, replica_groups=mesh['cfg'=2,'rs'=32,'tp'=8] {'tp'}, dimensions={0}, use_global_device_ids=true | all-gather | bytes 82944 | tf_op jit(solution)/shard_map/all_gather | solution.py:152
  51.2 616.4 %all-gather.2 = f32[256,36,16]{1,2,0:T(8,128)S(1)} all-gather(f32[1,36,16]{1,2,0:T(8,128)S(1)} %fusion.30), channel_id=1, replica_groups=mesh['cfg'=2,'rs'=32,'tp'=8] {'rs','tp'}, dimensions={0}, use_global_device_ids=true | all-gather | bytes 592128 | tf_op jit(solution)/shard_map/all_gather | solution.py:163
  668.3 2.4 reshape.288
  670.7 1.2 copy.101
  672.6 2.1 add.318
  674.7 4.0 add.319
  678.7 2.1 mul.284
  680.8 4.1 mul.285
  685.0 4.1 fusion.4
  690.2 1.9 collective-permute-start
  692.1 0.8 fusion.93
  692.9 0.8 copy.78
  694.1 1.3 fusion.96
  695.4 0.8 fusion.34
  696.1 2.2 pad_maximum_fusion
  698.3 2.0 copy.84
  700.4 2.1 collective-permute-start.1
  702.5 1.5 fusion.94
  704.2 0.8 copy.82
  705.6 26.2 %collective-permute-done.1 = bf16[512,2,288]{0,2,1:T(8,128)(2,1)} collective-permute-done((bf16[512,2,288]{0,2,1:T(8,128)(2,1)}, bf16[512,2,288]{0,2,1:T(8,128)(2,1)}, u32[]{:S(2)}, u32[]{:S(2)}) %collective-permute-start.1) | collective-permute-done | bytes 589856 | tf_op jit(solution)/shard_map/ppermute | solution.py:15
  731.8 1.1 fusion.92
  735.8 1.5 convolution_convert_fusion
  737.4 2.0 mul.280
  739.4 4.1 mul.306
  743.5 2.1 add.339
  745.6 4.0 add.340
  749.6 2.0 mul.311
  751.6 4.1 mul.312
  755.7 133.1 %all-reduce.2.cloned.1.call-done = bf16[512,1152]{1,0:T(8,128)(2,1)} async-done(((bf16[512,1152]{1,0:T(8,128)(2,1)}), bf16[512,1152]{1,0:T(8,128)(2,1)}) %all-reduce.2.cloned.1.call-update) | async-done | bytes 1179664 | tf_op jit(solution)/shard_map/psum | solution.py:176
  888.8 3.2 fusion.86
  892.0 1.4 copy-done.2
  894.1 6.4 convolution_convert_fusion.1
  900.8 4.0 reshape.270
  905.1 0.9 constant_dynamic-slice_fusion
  906.0 2.2 reshape.280
  908.3 97.9 %all-gather.5.cloned.1.call-done = bf16[4096,1152]{1,0:T(8,128)(2,1)} async-done(((bf16[512,1152]{1,0:T(8,128)(2,1)}), bf16[4096,1152]{1,0:T(8,128)(2,1)}) %all-gather.5.cloned.1.call-update) | async-done | bytes 9437200 | tf_op jit(solution)/shard_map/all_gather | solution.py:132
  1006.2 5.7 reduce_sum.109
  1011.9 2.2 reshape.283
  1014.2 1.6 fusion.84
  1016.9 3.6 collective-permute-start.2
  1020.8 1.7 collective-permute-done.2
  1022.5 0.7 multiply_add_fusion.1
  (122 shorter events, 10.7 us)
Async XLA Ops:
  6.5 887.2 %copy-start = (bf16[1,576,1152]{2,1,0:T(8,128)(2,1)S(1)}, bf16[1,576,1152]{2,1,0:T(8,128)(2,1)}, u32[]{:S(2)}) copy-start(bf16[1,576,1152]{2,1,0:T(8,128)(2,1)} %param.36) | copy-start | bytes 3981316
  6.5 882.3 %all-reduce.2.cloned.1.call-start = ((), (), s32[]{:S(2)}) async-start(), calls=%async_computation | async-start | bytes 2359296 | tf_op jit(solution)/shard_map/psum | solution.py:176
  12.0 6.3 copy-start.3
  14.2 4.1 copy-start.10
  14.2 4.2 copy-start.11
  14.2 4.2 copy-start.14
  22.1 1.4 copy-start.1
  22.1 1.8 copy-start.21
  22.1 2.0 copy-start.17
  22.1 2.2 copy-start.24
  22.1 2.3 copy-start.8
  22.1 28.9 %copy-start.23 = (bf16[36,1152]{1,0:T(8,128)(2,1)S(1)}, bf16[36,1152]{1,0:T(8,128)(2,1)}, u32[]{:S(2)}) copy-start(bf16[36,1152]{1,0:T(8,128)(2,1)} %param.28) | copy-start | bytes 248836
  22.1 28.9 %copy-start.27 = (f32[36]{0:T(128)S(1)}, f32[36]{0:T(128)}, u32[]{:S(2)}) copy-start(f32[36]{0:T(128)} %param.29) | copy-start | bytes 436
  680.8 4.1 copy-start.19
  680.8 4.2 copy-start.6
  690.2 5.9 copy-start.5
  690.2 5.9 collective-permute-start
  700.4 31.5 %collective-permute-start.1 = (bf16[512,2,288]{0,2,1:T(8,128)(2,1)}, bf16[512,2,288]{0,2,1:T(8,128)(2,1)}, u32[]{:S(2)}, u32[]{:S(2)}) collective-permute-start(bf16[512,2,288]{0,2,1:T(8,128)(2,1)} %copy.84), channel_id=1, source_target_pairs={{0,16},{8,24},{16,0},{24,8},{32,48},{40,56},{48,32},{56,40},{64,80... | collective-permute-start | bytes 1769480 | tf_op jit(solution)/shard_map/ppermute | solution.py:15
  732.9 1.2 copy-start.13
  734.1 1.0 copy-start.9
  734.5 1.3 copy-start.7
  735.4 1.9 copy-start.12
  737.3 268.9 %all-gather.5.cloned.1.call-start = ((), (), s32[]{:S(2)}) async-start(), calls=%async_computation.1 | async-start | bytes 10616832 | tf_op jit(solution)/shard_map/all_gather | solution.py:132
  739.4 4.1 copy-start.15
  751.6 4.1 copy-start.20
  892.0 1.4 copy-start.2
  892.0 2.2 copy-start.22
  894.1 6.5 copy-start.18
  900.8 4.0 copy-start.16
  900.8 4.1 copy-start.26
  900.8 5.2 copy-start.4
  1011.9 4.5 copy-start.25
  1011.9 4.5 copy-start.28
  1016.9 5.5 collective-permute-start.2
Sparse Core Ops, SparseCore 0:
  737.4 151.3 all-reduce.1
  900.7 105.4 all-gather.4
